TPU v7x, 32 devices: a whole 2x2x4 slice. The times are simulated.
32 devices in a mesh: group: 2 (over y), ctx: 8 (over z, x), tp: 2 (over core).
Axes of the slice: x: 2, y: 2, z: 4, core: 2. Of those that a mesh axis runs over, the one named last changes fastest.
Arguments:
- queries: bfloat16 [2048, 4096], P(('group', 'ctx'), 'tp'), parts along dimension 0, may hold values from -1.796875 to 1.796875
- key_rows: bfloat16 [2048, 4096], P(('group', 'ctx'), 'tp'), parts along dimension 0, may hold values from -1.796875 to 1.796875
- value_rows: bfloat16 [2048, 4096], P(('group', 'ctx'), 'tp'), parts along dimension 0, may hold values from -6 to 6
- out_grad: bfloat16 [2048, 4096], P(('group', 'ctx', 'tp')), parts along dimension 0, may hold values from -0.119628906 to 0.119628906
- log_decay: float32 [2048, 32], P(('group', 'ctx'), 'tp'), parts along dimension 0, may hold values from -0.8 to 0
- doc_ids: int32 [32], P('group'), parts along dimension 0, may hold values from 0 to 3, never falling along the last dimension, each value on 1 to 8 neighbouring positions
Outputs:
- key_grad: bfloat16 [2048, 4096], P(('group', 'ctx'), 'tp'), parts along dimension 0
- value_grad: bfloat16 [2048, 4096], P(('group', 'ctx'), 'tp'), parts along dimension 0
There are 2 independent parts, one for each index of `group`. A program takes and returns all parts, laid end to end along the dimension named above; each array names one. Nothing has to cross between parts.
Inputs may be any that keep to these rules, and one draw needn't show every extreme that they name: `doc_ids`: one entry per block of 64 positions; each document covers 1 to 8 consecutive blocks, one exactly 8; document numbers never fall.
All inputs are finite; a program needn't handle non-finite values.
Results may differ from a plain program's by a relative error of at most 0.0056.
Values may be sent and summed in bfloat16 or wider, within the bound.
A program may use at most 64 MiB of HBM per device.

v0:
```python
import jax
import jax.numpy as jnp
from jax import lax
from jax.sharding import PartitionSpec as P

BLOCK = 64


def shifted(value, axis, steps):
    count = lax.axis_size(axis)
    leading, last = (max(0, -steps), min(count, count - steps))
    return lax.ppermute(value, axis, [(source, source + steps) for source in range(leading, last)])


def product(pattern, first_op, second_op):
    return jnp.einsum(pattern, first_op, second_op, preferred_element_type=jnp.float32)


def span_terms(queries, key_rows, value_rows, grad_rows, log_decay, doc_rows, prev_doc):
    row_count, head_count = log_decay.shape
    head_size = queries.shape[1] // head_count
    query_heads = queries.reshape(row_count, head_count, head_size)
    key_heads = key_rows.reshape(row_count, head_count, head_size)
    value_heads = value_rows.reshape(row_count, head_count, head_size)
    grad_heads = grad_rows.reshape(row_count, head_count, head_size)
    cumulative = jnp.cumsum(log_decay.T, axis=1)
    spread = cumulative[:, :, None] - cumulative[:, None, :]
    position = jnp.arange(row_count)
    allowed = (position[:, None] >= position[None, :]) & (doc_rows[:, None] == doc_rows[None, :])
    weight = jnp.where(allowed[None], jnp.exp(jnp.minimum(spread, 0.0)), 0.0)
    grad_value = product("thd,shd->hts", grad_heads, value_heads)
    query_key = product("thd,shd->hts", query_heads, key_heads)
    mixed_gv = (weight * grad_value).astype(jnp.bfloat16)
    mixed_qk = (weight * query_key).astype(jnp.bfloat16)
    key_inner = product("hts,thd->shd", mixed_gv, query_heads)
    value_inner = product("hts,thd->shd", mixed_qk, grad_heads)
    first_doc = doc_rows[0]
    last_doc = doc_rows[-1]
    linked = (prev_doc == first_doc).astype(jnp.float32)
    lead_mask = (doc_rows == first_doc).astype(jnp.float32)
    scaling = jnp.exp(cumulative).T * lead_mask[:, None]
    scaled = (query_heads * scaling[:, :, None]).astype(jnp.bfloat16)
    state = product("thi,thj->hij", scaled, grad_heads) * linked
    through = linked * (first_doc == last_doc).astype(jnp.float32)
    factor = through * jnp.exp(cumulative[:, -1])
    tail_mask = (doc_rows == last_doc).astype(jnp.float32)
    weight_in = jnp.exp(cumulative[:, -1:] - cumulative) * tail_mask[None, :]
    return (key_inner, value_inner, state, factor, weight_in)


def apply_state(incoming, key_rows, value_rows, weight_in, key_inner, value_inner):
    row_count = key_rows.shape[0]
    head_count, head_size = (incoming.shape[0], incoming.shape[1])
    key_heads = key_rows.reshape(row_count, head_count, head_size)
    value_heads = value_rows.reshape(row_count, head_count, head_size)
    rounded = incoming.astype(jnp.bfloat16)
    to_keys = product("hij,shj->shi", rounded, value_heads)
    to_values = product("hij,shi->shj", rounded, key_heads)
    scaling = weight_in.T[:, :, None]
    key_grad = (
        (key_inner + scaling * to_keys)
        .astype(jnp.bfloat16)
        .reshape(row_count, head_count * head_size)
    )
    value_grad = (
        (value_inner + scaling * to_values)
        .astype(jnp.bfloat16)
        .reshape(row_count, head_count * head_size)
    )
    return (key_grad, value_grad)


def doubling_states(factor, state):
    ctx_count = lax.axis_size("ctx")
    gathered_state = jnp.zeros_like(state)
    gathered_decay = jnp.ones_like(factor)
    distance = 1
    while distance < ctx_count:
        outgoing_state = state + factor[:, None, None] * gathered_state
        outgoing_decay = factor * gathered_decay
        farther = shifted((outgoing_decay, outgoing_state), "ctx", -distance)
        gathered_state = gathered_state + gathered_decay[:, None, None] * farther[1]
        gathered_decay = gathered_decay * farther[0]
        distance = distance * 2
    return gathered_state


def per_device(queries, key_rows, value_rows, out_grad, log_decay, doc_ids):
    row_count, feature_count = queries.shape
    grad_rows = lax.all_to_all(out_grad, "tp", split_axis=1, concat_axis=0, tiled=True)
    block_count = row_count // BLOCK
    first_block = lax.axis_index("ctx") * block_count
    own_blocks = lax.dynamic_slice_in_dim(doc_ids, first_block, block_count)
    doc_rows = jnp.repeat(own_blocks, BLOCK)
    prev_doc = jnp.where(first_block > 0, doc_ids[jnp.maximum(first_block - 1, 0)], -1)
    key_inner, value_inner, state, factor, weight_in = span_terms(
        queries, key_rows, value_rows, grad_rows, log_decay, doc_rows, prev_doc
    )
    incoming = doubling_states(factor, state)
    return apply_state(incoming, key_rows, value_rows, weight_in, key_inner, value_inner)


def solution(mesh):
    placed = (
        P(("group", "ctx"), "tp"),
        P(("group", "ctx"), "tp"),
        P(("group", "ctx"), "tp"),
        P(("group", "ctx", "tp"), None),
        P(("group", "ctx"), "tp"),
        P("group"),
    )
    return jax.shard_map(
        per_device,
        mesh=mesh,
        in_specs=placed,
        out_specs=(P(("group", "ctx"), "tp"), P(("group", "ctx"), "tp")),
        check_vma=False,
    )
```

profile of v0, /device:TPU:0, one launch (start us, length us, event | category | flops | bytes accessed | tf_op | source)
XLA Modules:
  0.0 128.8 jit_solution(10038552793996100235)
XLA Ops:
  0.6 1.9 %copy.54 = bf16[8,2,8,2048]{3,2,0,1:T(8,128)(2,1)} copy(bf16[8,2,8,2048]{3,2,1,0:T(8,128)(2,1)} %bitcast.79) | data formatting | bytes 1048576 | tf_op jit(solution)/shard_map/all_to_all | solution.py:90
  2.6 3.5 %all-to-all-start = ((bf16[64,2,2048]{2,0,1:T(8,128)(2,1)}), bf16[64,2,2048]{2,0,1:T(8,128)(2,1)S(1)}, u32[]{:S(2)}, u32[]{:S(2)}) async-start(bf16[64,2,2048]{2,0,1:T(8,128)(2,1)} %bitcast.73), calls=%async_computation | async-start | bytes 1048576 | tf_op jit(solution)/shard_map/all_to_all | solution.py:90
  6.1 0.6 copy-done.3
  7.0 0.6 fusion.32
  7.6 1.3 %compare_convert_fusion.1 = (f32[128]{0:T(128)S(1)}, f32[128]{0:T(128)S(1)}) fusion(s32[128]{0:T(128)S(1)} %eq.45, s32[]{:T(128)} %bitcast.3, s32[]{:T(128)} %bitcast.5), kind=kLoop, calls=%fused_computation.46 | loop fusion | flops 512 | bytes 1544 | tf_op jit(solution)/shard_map/convert_element_type | solution.py:46
  10.6 0.6 dynamic_slice.7
  13.1 0.6 copy-done.1
  14.1 0.5 broadcast_add_fusion
  14.5 1.3 %collective-permute-start = (f32[16,128,128]{2,1,0:T(8,128)S(1)}, f32[16,128,128]{2,1,0:T(8,128)S(1)}, u32[]{:S(2)}, u32[]{:S(2)}) collective-permute-start(f32[16,128,128]{2,1,0:T(8,128)S(1)} %get-tuple-element.14), channel_id=1, source_target_pairs={{2,0},{4,2},{6,4},{8,6},{10,8},{12,10},{14,12},{3,1},{5,3},{7,5},{... | collective-permute-start | bytes 3145736 | tf_op jit(solution)/shard_map/ppermute | solution.py:12
  15.8 27.4 %collective-permute-done = f32[16,128,128]{2,1,0:T(8,128)S(1)} collective-permute-done((f32[16,128,128]{2,1,0:T(8,128)S(1)}, f32[16,128,128]{2,1,0:T(8,128)S(1)}, u32[]{:S(2)}, u32[]{:S(2)}) %collective-permute-start) | collective-permute-done | bytes 1048608 | tf_op jit(solution)/shard_map/ppermute | solution.py:12
  43.4 1.3 %collective-permute-start.2 = (f32[16,128,128]{2,1,0:T(8,128)S(1)}, f32[16,128,128]{2,1,0:T(8,128)S(1)}, u32[]{:S(2)}, u32[]{:S(2)}) collective-permute-start(f32[16,128,128]{2,1,0:T(8,128)S(1)} %multiply_add_fusion.2), channel_id=1, source_target_pairs={{4,0},{6,2},{8,4},{10,6},{12,8},{14,10},{5,1},{7,3},{9,5},{11,7},{... | collective-permute-start | bytes 3145736 | tf_op jit(solution)/shard_map/ppermute | solution.py:12
  44.7 1.3 %collective-permute-start.1 = (f32[16]{0:T(128)S(1)}, f32[16]{0:T(128)S(1)}, u32[]{:S(2)}, u32[]{:S(2)}) collective-permute-start(f32[16]{0:T(128)S(1)} %get-tuple-element.7), channel_id=1, source_target_pairs={{2,0},{4,2},{6,4},{8,6},{10,8},{12,10},{14,12},{3,1},{5,3},{7,5},{... | collective-permute-start | bytes 200 | tf_op jit(solution)/shard_map/ppermute | solution.py:12
  46.0 4.8 %collective-permute-done.1 = f32[16]{0:T(128)S(1)} collective-permute-done((f32[16]{0:T(128)S(1)}, f32[16]{0:T(128)S(1)}, u32[]{:S(2)}, u32[]{:S(2)}) %collective-permute-start.1) | collective-permute-done | bytes 96 | tf_op jit(solution)/shard_map/ppermute | solution.py:12
  50.8 19.5 %collective-permute-done.2 = f32[16,128,128]{2,1,0:T(8,128)S(1)} collective-permute-done((f32[16,128,128]{2,1,0:T(8,128)S(1)}, f32[16,128,128]{2,1,0:T(8,128)S(1)}, u32[]{:S(2)}, u32[]{:S(2)}) %collective-permute-start.2) | collective-permute-done | bytes 1048608 | tf_op jit(solution)/shard_map/ppermute | solution.py:12
  70.5 1.3 %collective-permute-start.4 = (f32[16,128,128]{2,1,0:T(8,128)S(1)}, f32[16,128,128]{2,1,0:T(8,128)S(1)}, u32[]{:S(2)}, u32[]{:S(2)}) collective-permute-start(f32[16,128,128]{2,1,0:T(8,128)S(1)} %multiply_add_fusion), channel_id=1, source_target_pairs={{8,0},{10,2},{12,4},{14,6},{9,1},{11,3},{13,5},{15,7},{24,16},{26,... | collective-permute-start | bytes 3145736 | tf_op jit(solution)/shard_map/ppermute | solution.py:12
  71.9 1.3 %collective-permute-start.3 = (f32[16]{0:T(128)S(1)}, f32[16]{0:T(128)S(1)}, u32[]{:S(2)}, u32[]{:S(2)}) collective-permute-start(f32[16]{0:T(128)S(1)} %mul.140), channel_id=1, source_target_pairs={{4,0},{6,2},{8,4},{10,6},{12,8},{14,10},{5,1},{7,3},{9,5},{11,7},{... | collective-permute-start | bytes 200 | tf_op jit(solution)/shard_map/ppermute | solution.py:12
  73.2 4.1 %collective-permute-done.3 = f32[16]{0:T(128)S(1)} collective-permute-done((f32[16]{0:T(128)S(1)}, f32[16]{0:T(128)S(1)}, u32[]{:S(2)}, u32[]{:S(2)}) %collective-permute-start.3) | collective-permute-done | bytes 96 | tf_op jit(solution)/shard_map/ppermute | solution.py:12
  77.3 42.6 %collective-permute-done.4 = f32[16,128,128]{2,1,0:T(8,128)S(1)} collective-permute-done((f32[16,128,128]{2,1,0:T(8,128)S(1)}, f32[16,128,128]{2,1,0:T(8,128)S(1)}, u32[]{:S(2)}, u32[]{:S(2)}) %collective-permute-start.4) | collective-permute-done | bytes 1048608 | tf_op jit(solution)/shard_map/ppermute | solution.py:12
  120.2 0.5 fusion.2
  120.8 1.6 %fusion.7 = bf16[128,16,128]{0,2,1:T(8,128)(2,1)} fusion(f32[128,16,128]{0,2,1:T(8,128)S(1)} %fusion.2, bf16[128,16,128]{0,2,1:T(8,128)(2,1)S(1)} %copy.21, bf16[128,16,128]{0,2,1:T(8,128)(2,1)S(1)} %bitcast.77, f32[16,128]{1,0:T(8,128)S(1)} %reduce_window_sum.11, pred[128,128]{1,0:T(8,128)(4,1)S(1)} %fusion.29, bf16[128,2048]{1,0:T(8,128)(2,1)S(1)} %copy-done), kind=kOutput, calls=%fused_computation.14 | convolution fusion | flops 136052736 | bytes 3170304 | tf_op jit(solution)/shard_map/hts,thd->shd/dot_general | solution.py:16
  122.3 2.0 %copy.25 = bf16[128,2048]{1,0:T(8,128)(2,1)} copy(bf16[128,2048]{0,1:T(8,128)(2,1)} %bitcast.81) | data formatting | bytes 1048576
  124.4 1.5 %fusion.3 = f32[128,16,128]{0,2,1:T(8,128)S(1)} fusion(bf16[16,128,128]{2,1,0:T(8,128)(2,1)S(1)} %add_convert_fusion, f32[128,16]{0,1:T(8,128)S(1)} %get-tuple-element.8, bf16[128,2048]{1,0:T(8,128)(2,1)} %param.8), kind=kOutput, calls=%fused_computation.8 | convolution fusion | flops 67371008 | bytes 2105344 | tf_op jit(solution)/shard_map/hij,shj->shi/dot_general | solution.py:16
  125.9 1.8 %fusion.6 = bf16[128,16,128]{0,2,1:T(8,128)(2,1)S(1)} fusion(f32[128,16,128]{0,2,1:T(8,128)S(1)} %fusion.3, bf16[128,16,128]{0,2,1:T(8,128)(2,1)S(1)} %bitcast.78, bf16[128,16,128]{0,2,1:T(8,128)(2,1)S(1)} %copy.21, f32[16,128]{1,0:T(8,128)S(1)} %reduce_window_sum.11, pred[128,128]{1,0:T(8,128)(4,1)S(1)} %fusion.29, bf16[128,2048]{1,0:T(8,128)(2,1)} %param.8), kind=kOutput, calls=%fused_computation.13 | convolution fusion | flops 136052736 | bytes 3170304 | tf_op jit(solution)/shard_map/hts,thd->shd/dot_general | solution.py:16
  127.7 1.0 copy.24
  (23 shorter events, 2.5 us)
Async XLA Ops:
  0.6 119.6 %copy-start = (bf16[128,2048]{1,0:T(8,128)(2,1)S(1)}, bf16[128,2048]{1,0:T(8,128)(2,1)}, u32[]{:S(2)}) copy-start(bf16[128,2048]{1,0:T(8,128)(2,1)} %param.7) | copy-start | bytes 1572868
  2.6 9.9 %all-to-all-start = ((bf16[64,2,2048]{2,0,1:T(8,128)(2,1)}), bf16[64,2,2048]{2,0,1:T(8,128)(2,1)S(1)}, u32[]{:S(2)}, u32[]{:S(2)}) async-start(bf16[64,2,2048]{2,0,1:T(8,128)(2,1)} %bitcast.73), calls=%async_computation | async-start | bytes 1048576 | tf_op jit(solution)/shard_map/all_to_all | solution.py:90
  6.1 0.7 copy-start.3
  7.6 2.6 %copy-start.2 = (f32[128,16]{0,1:T(8,128)S(1)}, f32[128,16]{0,1:T(8,128)}, u32[]{:S(2)}) copy-start(f32[128,16]{0,1:T(8,128)} %param.10) | copy-start | bytes 24580
  12.6 1.0 copy-start.1
  14.5 28.7 %collective-permute-start = (f32[16,128,128]{2,1,0:T(8,128)S(1)}, f32[16,128,128]{2,1,0:T(8,128)S(1)}, u32[]{:S(2)}, u32[]{:S(2)}) collective-permute-start(f32[16,128,128]{2,1,0:T(8,128)S(1)} %get-tuple-element.14), channel_id=1, source_target_pairs={{2,0},{4,2},{6,4},{8,6},{10,8},{12,10},{14,12},{3,1},{5,3},{7,5},{... | collective-permute-start | bytes 3145736 | tf_op jit(solution)/shard_map/ppermute | solution.py:12
  43.4 26.9 %collective-permute-start.2 = (f32[16,128,128]{2,1,0:T(8,128)S(1)}, f32[16,128,128]{2,1,0:T(8,128)S(1)}, u32[]{:S(2)}, u32[]{:S(2)}) collective-permute-start(f32[16,128,128]{2,1,0:T(8,128)S(1)} %multiply_add_fusion.2), channel_id=1, source_target_pairs={{4,0},{6,2},{8,4},{10,6},{12,8},{14,10},{5,1},{7,3},{9,5},{11,7},{... | collective-permute-start | bytes 3145736 | tf_op jit(solution)/shard_map/ppermute | solution.py:12
  44.7 6.1 %collective-permute-start.1 = (f32[16]{0:T(128)S(1)}, f32[16]{0:T(128)S(1)}, u32[]{:S(2)}, u32[]{:S(2)}) collective-permute-start(f32[16]{0:T(128)S(1)} %get-tuple-element.7), channel_id=1, source_target_pairs={{2,0},{4,2},{6,4},{8,6},{10,8},{12,10},{14,12},{3,1},{5,3},{7,5},{... | collective-permute-start | bytes 200 | tf_op jit(solution)/shard_map/ppermute | solution.py:12
  70.5 49.4 %collective-permute-start.4 = (f32[16,128,128]{2,1,0:T(8,128)S(1)}, f32[16,128,128]{2,1,0:T(8,128)S(1)}, u32[]{:S(2)}, u32[]{:S(2)}) collective-permute-start(f32[16,128,128]{2,1,0:T(8,128)S(1)} %multiply_add_fusion), channel_id=1, source_target_pairs={{8,0},{10,2},{12,4},{14,6},{9,1},{11,3},{13,5},{15,7},{24,16},{26,... | collective-permute-start | bytes 3145736 | tf_op jit(solution)/shard_map/ppermute | solution.py:12
  71.9 5.5 %collective-permute-start.3 = (f32[16]{0:T(128)S(1)}, f32[16]{0:T(128)S(1)}, u32[]{:S(2)}, u32[]{:S(2)}) collective-permute-start(f32[16]{0:T(128)S(1)} %mul.140), channel_id=1, source_target_pairs={{4,0},{6,2},{8,4},{10,6},{12,8},{14,10},{5,1},{7,3},{9,5},{11,7},{... | collective-permute-start | bytes 200 | tf_op jit(solution)/shard_map/ppermute | solution.py:12
where the time goes:
time: 129 us
  waiting for transfers between devices  98.3 us (76%)
  starting transfers between devices  9.95 us (8%)
  local copies, waits for them, and re-layouts  8.66 us (7%)
  matrix products  5.95 us (5%)
  between operations  3.39 us (3%)
  other arithmetic  2.49 us (2%)
    ppermute x5, waiting for transfers between devices, shifted(): lax.ppermute(value, axis, [(source, source + steps) for source in range(l...  98.3 us
    ppermute x5, starting transfers between devices, shifted(): lax.ppermute(value, axis, [(source, source + steps) for source in range(l...  6.46 us
    dot_general x5, matrix products, product(): jnp.einsum(pattern, first_op, second_op, preferred_element_type=jnp.float32)  5.95 us
    unnamed x11, local copies, waits for them, and re-layouts  4.4 us
    all_to_all x1, starting transfers between devices, per_device(): lax.all_to_all(out_grad, 'tp', split_axis=1, concat_axis=0, tiled=True)  3.49 us
  transfers between devices with their start and end apart: 6, of which 5 were waited for; matrix products, arithmetic and copies ran while one was open for 3% of the time, Pallas kernels for 0%

commit v1 on v0

v1 whole, which is shorter than its diff:
```python
import functools

import jax
import jax.numpy as jnp
from jax import lax
from jax.experimental import pallas as pl
from jax.experimental.pallas import tpu as pltpu
from jax.sharding import PartitionSpec as P

BLOCK = 64
DH = 128
MESH = pl.DeviceIdType.MESH


def dot(a, b, dims):
    return lax.dot_general(a, b, (dims, ((), ())), preferred_element_type=jnp.float32)


NN = ((1,), (0,))
NT = ((1,), (1,))


def kernel(ctx_count, heads, docs, decay, q_hbm, k_hbm, v_hbm, og_hbm, dk, dv,
           q, k, v, g, cum, lead_row, tail_row, factor, factor_other, mine, other, sent, later,
           load_sem, swap_sem, fac_sem, pair_send, pair_recv, chain_send, chain_recv):
    rows = q.shape[0]
    half = og_hbm.shape[0]
    width = q.shape[1]
    group, ctx, tp = lax.axis_index("group"), lax.axis_index("ctx"), lax.axis_index("tp")
    odd = lax.rem(ctx, 2)
    pair = (group, ctx + 1 - 2 * odd, tp)
    core = (group, ctx, 1 - tp)
    before = (group, ctx - 2, tp)
    after = (group, ctx + 2, tp)
    has_before = ctx >= 2
    has_after = ctx < ctx_count - 2

    loads = [pltpu.make_async_copy(src, dst, load_sem.at[i])
             for i, (src, dst) in enumerate(((q_hbm, q), (k_hbm, k), (v_hbm, v)))]
    own_rows = pl.ds(pl.multiple_of(tp * half, half), half)
    loads.append(pltpu.make_async_copy(
        og_hbm.at[:, pl.ds(pl.multiple_of(tp * width, width), width)], g.at[own_rows, :], load_sem.at[3]))
    for copy in loads:
        copy.start()

    barrier = pltpu.get_barrier_semaphore()
    for peer in (pair, core):
        pl.semaphore_signal(barrier, inc=1, device_id=peer, device_id_type=MESH)

    @pl.when(has_before)
    def _():
        pl.semaphore_signal(barrier, inc=1, device_id=before, device_id_type=MESH)

    @pl.when(has_after)
    def _():
        pl.semaphore_signal(barrier, inc=1, device_id=after, device_id_type=MESH)

    pl.semaphore_wait(barrier, 2 + has_before.astype(jnp.int32) + has_after.astype(jnp.int32))

    swap = pltpu.make_async_remote_copy(
        src_ref=og_hbm.at[:, pl.ds(pl.multiple_of((1 - tp) * width, width), width)],
        dst_ref=g.at[own_rows, :], send_sem=swap_sem.at[0], recv_sem=swap_sem.at[1],
        device_id=core, device_id_type=MESH)
    swap.start()

    blocks = rows // BLOCK
    doc_list = [docs[ctx * blocks + b] for b in range(blocks)]
    first, last = doc_list[0], doc_list[-1]
    prev = docs[jnp.maximum(ctx * blocks - 1, 0)]
    linked = jnp.where((ctx > 0) & (prev == first), 1.0, 0.0).astype(jnp.float32)
    through = jnp.where(first == last, linked, 0.0).astype(jnp.float32)

    def doc_of(position):
        doc = jnp.full(position.shape, first, jnp.int32)
        for b in range(1, blocks):
            doc = jnp.where(position >= b * BLOCK, doc_list[b], doc)
        return doc

    lane = lax.broadcasted_iota(jnp.int32, (heads, rows), 1)
    total = decay[...]
    step = 1
    while step < rows:
        total = total + jnp.where(lane >= step, pltpu.roll(total, step, 1), 0.0)
        step *= 2
    lane_doc = doc_of(lane)
    ending = jnp.broadcast_to(total[:, rows - 1:rows], (heads, rows))
    cum[...] = total
    lead_row[...] = jnp.where(lane_doc == first, jnp.exp(total) * linked, 0.0)
    tail_row[...] = jnp.where(lane_doc == last, jnp.exp(ending - total), 0.0)
    factor[...] = jnp.exp(ending) * through
    fac_copy = pltpu.make_async_remote_copy(
        src_ref=factor, dst_ref=factor_other, send_sem=fac_sem.at[0], recv_sem=fac_sem.at[1],
        device_id=pair, device_id_type=MESH)
    fac_copy.start()

    def pair_copy(h):
        return pltpu.make_async_remote_copy(
            src_ref=mine.at[h], dst_ref=other.at[h], send_sem=pair_send.at[h], recv_sem=pair_recv.at[h],
            device_id=pair, device_id_type=MESH)

    def chain_copy(h):
        return pltpu.make_async_remote_copy(
            src_ref=sent.at[h], dst_ref=later.at[h], send_sem=chain_send.at[h], recv_sem=chain_recv.at[h],
            device_id=before, device_id_type=MESH)

    def columns(h):
        return pl.ds(pl.multiple_of(h * DH, DH), DH)

    for copy in loads:
        copy.wait()
    swap.wait()

    def state_step(h, carry):
        turned = q[:, columns(h)].astype(jnp.float32).T
        scaled = (turned * lead_row[pl.ds(h, 1), :]).astype(jnp.bfloat16)
        mine[h] = dot(scaled, g[:, columns(h)], NN).astype(mine.dtype)
        pair_copy(h).start()
        return carry

    lax.fori_loop(0, heads, state_step, 0, unroll=2)
    fac_copy.wait()

    key_at = lax.broadcasted_iota(jnp.int32, (rows, rows), 0)
    query_at = lax.broadcasted_iota(jnp.int32, (rows, rows), 1)
    allowed = (query_at >= key_at) & (doc_of(query_at) == doc_of(key_at))
    even = odd == 0

    def head_step(h, carry):
        cols = columns(h)
        qh, kh, vh, gh = q[:, cols], k[:, cols], v[:, cols], g[:, cols]
        along = jnp.broadcast_to(cum[pl.ds(h, 1), :], (rows, rows))
        weight = jnp.where(allowed, jnp.exp(jnp.minimum(along - along.T, 0.0)), 0.0)
        mixed_gv = (weight * dot(vh, gh, NT)).astype(jnp.bfloat16)
        mixed_qk = (weight * dot(kh, qh, NT)).astype(jnp.bfloat16)
        key_inner = dot(mixed_gv, qh, NN)
        value_inner = dot(mixed_qk, gh, NN)
        scale = jnp.broadcast_to(tail_row[pl.ds(h, 1), :], (rows, rows)).T

        pair_copy(h).wait_recv()
        own_state, pair_state = mine[h].astype(jnp.float32), other[h].astype(jnp.float32)
        own_factor, pair_factor = factor[pl.ds(h, 1), :], factor_other[pl.ds(h, 1), :]
        state_even = jnp.where(even, own_state, pair_state)
        state_odd = jnp.where(even, pair_state, own_state)
        factor_even = jnp.where(even, own_factor, pair_factor)

        @pl.when(has_after)
        def _():
            chain_copy(h).wait_recv()

        incoming = jnp.where(has_after, later[h].astype(jnp.float32), 0.0)

        @pl.when(has_before)
        def _():
            sent[h] = (state_even + factor_even * state_odd
                       + (own_factor * pair_factor) * incoming).astype(sent.dtype)
            chain_copy(h).start()

        state_in = jnp.where(even, pair_state + pair_factor * incoming, incoming).astype(jnp.bfloat16)
        dk[:, cols] = (key_inner + scale * dot(vh, state_in, NT)).astype(dk.dtype)
        dv[:, cols] = (value_inner + scale * dot(kh, state_in, NN)).astype(dv.dtype)
        return carry

    lax.fori_loop(0, heads, head_step, 0)

    def drain(h, carry):
        pair_copy(h).wait_send()

        @pl.when(has_before)
        def _():
            chain_copy(h).wait_send()

        return carry

    lax.fori_loop(0, heads, drain, 0)


def solution(mesh):
    ctx_count = mesh.shape["ctx"]
    wire = jnp.bfloat16 if ctx_count <= 8 else jnp.float32

    def per_device(queries, key_rows, value_rows, out_grad, log_decay, doc_ids):
        rows, features = queries.shape
        heads = log_decay.shape[1]
        anywhere = pl.BlockSpec(memory_space=pl.ANY)
        in_vmem = pl.BlockSpec(memory_space=pltpu.VMEM)
        wide = pltpu.VMEM((rows, features), jnp.bfloat16)
        small = pltpu.VMEM((heads, rows), jnp.float32)
        states = pltpu.VMEM((heads, DH, DH), wire)
        many = pltpu.SemaphoreType.DMA((heads,))
        shape = jax.ShapeDtypeStruct((rows, features), jnp.bfloat16)
        return tuple(pl.pallas_call(
            functools.partial(kernel, ctx_count, heads),
            out_shape=(shape, shape),
            in_specs=[pl.BlockSpec(memory_space=pltpu.SMEM), in_vmem] + [anywhere] * 4,
            out_specs=(in_vmem, in_vmem),
            scratch_shapes=[wide] * 4 + [small] * 5 + [states] * 4 + [
                pltpu.SemaphoreType.DMA((4,)), pltpu.SemaphoreType.DMA((2,)), pltpu.SemaphoreType.DMA((2,)),
                many, many, many, many],
            compiler_params=pltpu.CompilerParams(
                collective_id=0, has_side_effects=True, vmem_limit_bytes=63 << 20),
        )(doc_ids, log_decay.T, queries, key_rows, value_rows, out_grad))

    placed = (
        P(("group", "ctx"), "tp"),
        P(("group", "ctx"), "tp"),
        P(("group", "ctx"), "tp"),
        P(("group", "ctx", "tp"), None),
        P(("group", "ctx"), "tp"),
        P("group"),
    )
    return jax.shard_map(
        per_device,
        mesh=mesh,
        in_specs=placed,
        out_specs=(P(("group", "ctx"), "tp"), P(("group", "ctx"), "tp")),
        check_vma=False,
    )
```

time: 129 us -> 35.4 us (0.27)
  waiting for transfers between devices: 98.3 us -> 0 us
  Pallas kernels: 0 us -> 31.8 us
  starting transfers between devices: 9.95 us -> 0 us
  matrix products: 5.95 us -> 0 us
  local copies, waits for them, and re-layouts: 8.66 us -> 2.74 us
  between operations: 3.39 us -> 0.65 us
  other arithmetic: 2.49 us -> 0 us
    ppermute x5 -> x0, waiting for transfers between devices: 98.3 us -> none  [shifted(): lax.ppermute(value, axis, [(source, source + steps) for source in range(l...]
    pallas_call x0 -> x1, Pallas kernels: none -> 31.8 us  [per_device(): pl.pallas_call(functools.partial(kernel, ctx_count, heads), out_shape=(sh...]
    ppermute x5 -> x0, starting transfers between devices: 6.46 us -> none  [shifted(): lax.ppermute(value, axis, [(source, source + steps) for source in range(l...]
    dot_general x5 -> x0, matrix products: 5.95 us -> none  [product(): jnp.einsum(pattern, first_op, second_op, preferred_element_type=jnp.float32)]
    all_to_all x1 -> x0, starting transfers between devices: 3.49 us -> none  [per_device(): lax.all_to_all(out_grad, 'tp', split_axis=1, concat_axis=0, tiled=True)]
    all_to_all x1 -> x0, local copies, waits for them, and re-layouts: 1.94 us -> none  [per_device(): lax.all_to_all(out_grad, 'tp', split_axis=1, concat_axis=0, tiled=True)]
    unnamed x11 -> x4, local copies, waits for them, and re-layouts: 4.4 us -> 2.74 us
    convert_element_type x2 -> x0, other arithmetic: 1.58 us -> none  [the longest x1 1.29 us: span_terms(): tail_mask = (doc_rows == last_doc).astype(jnp.float32)]
  transfers between devices with their start and end apart: 6 -> 0, of which waited for: 5 -> 0; matrix products, arithmetic and copies ran while one was open for 3% -> 0% of each run, Pallas kernels for 0% -> 0%
where the time goes in v1:
time: 35.4 us; the launch traced here: 35.1 us
  Pallas kernels  31.8 us (90%)
  local copies, waits for them, and re-layouts  2.74 us (8%)
  between operations  0.65 us (2%)
    pallas_call x1, Pallas kernels, per_device(): pl.pallas_call(functools.partial(kernel, ctx_count, heads), out_shape=(sh...  31.8 us
    unnamed x4, local copies, waits for them, and re-layouts  2.74 us

profile of v1, /device:TPU:0, one launch (start us, length us, event | category | flops | bytes accessed | tf_op | source)
XLA Modules:
  0.0 35.1 jit_solution(14455751210185740948)
XLA Ops:
  0.6 31.8 %shard_map.77 = (bf16[128,2048]{1,0:T(8,128)(2,1)}, bf16[128,2048]{1,0:T(8,128)(2,1)}) custom-call(s32[16]{0:T(128)} %docs.1, f32[16,128]{1,0:T(8,128)} %bitcast.1, bf16[128,2048]{1,0:T(8,128)(2,1)} %q_hbm.1, bf16[128,2048]{1,0:T(8,128)(2,1)} %k_hbm.1, bf16[128,2048]{1,0:T(8,128)(2,1)} %v_hbm.1, bf16[64,4096]{1,0:T(8,128)(2,1)} %og_hbm.1), custom_call_target="tpu_custom_call" | custom-call | tf_op jit(solution)/shard_map/pallas_call | solution.py:191
  32.4 0.0 copy-start
  32.4 1.9 %copy.10 = bf16[128,2048]{1,0:T(8,128)(2,1)} copy(bf16[128,2048]{1,0:T(8,128)(2,1)} %get-tuple-element.4) | data formatting | bytes 1048576
  34.3 0.0 copy-done
  34.3 0.8 %copy.11 = bf16[128,2048]{1,0:T(8,128)(2,1)} copy(bf16[128,2048]{1,0:T(8,128)(2,1)S(1)} %copy-done) | data formatting | bytes 1048576
Async XLA Ops:
  32.4 2.0 %copy-start = (bf16[128,2048]{1,0:T(8,128)(2,1)S(1)}, bf16[128,2048]{1,0:T(8,128)(2,1)}, u32[]{:S(2)}) copy-start(bf16[128,2048]{1,0:T(8,128)(2,1)} %get-tuple-element.5) | copy-start | bytes 1572868

commit v2 on v1

--- a/solution.py
+++ b/solution.py
@@ -21,8 +21,9 @@
 
 
 def kernel(ctx_count, heads, docs, decay, q_hbm, k_hbm, v_hbm, og_hbm, dk, dv,
-           q, k, v, g, cum, lead_row, tail_row, factor, factor_other, mine, other, sent, later,
-           load_sem, swap_sem, fac_sem, pair_send, pair_recv, chain_send, chain_recv):
+           q, k, v, g, cum, lead_row, tail_row, factor, factor_other, mine, given, other, sent, later,
+           handed, back, key_inner, value_inner, allowed,
+           load_sem, swap_sem, fac_sem, pair_send, pair_recv, chain_send, chain_recv, back_send, back_recv):
     rows = q.shape[0]
     half = og_hbm.shape[0]
     width = q.shape[1]
@@ -93,15 +94,23 @@
         device_id=pair, device_id_type=MESH)
     fac_copy.start()
 
-    def pair_copy(h):
+    half_heads = heads // 2
+    own_base, pair_base = odd * half_heads, (1 - odd) * half_heads
+
+    def pair_copy(i):
         return pltpu.make_async_remote_copy(
-            src_ref=mine.at[h], dst_ref=other.at[h], send_sem=pair_send.at[h], recv_sem=pair_recv.at[h],
+            src_ref=given.at[i], dst_ref=other.at[i], send_sem=pair_send.at[i], recv_sem=pair_recv.at[i],
             device_id=pair, device_id_type=MESH)
 
-    def chain_copy(h):
+    def chain_copy(i):
         return pltpu.make_async_remote_copy(
-            src_ref=sent.at[h], dst_ref=later.at[h], send_sem=chain_send.at[h], recv_sem=chain_recv.at[h],
+            src_ref=sent.at[i], dst_ref=later.at[i], send_sem=chain_send.at[i], recv_sem=chain_recv.at[i],
             device_id=before, device_id_type=MESH)
+
+    def back_copy(i):
+        return pltpu.make_async_remote_copy(
+            src_ref=handed.at[i], dst_ref=back.at[i], send_sem=back_send.at[i], recv_sem=back_recv.at[i],
+            device_id=pair, device_id_type=MESH)
 
     def columns(h):
         return pl.ds(pl.multiple_of(h * DH, DH), DH)
@@ -110,68 +119,97 @@
         copy.wait()
     swap.wait()
 
-    def state_step(h, carry):
+    def state_of(h):
         turned = q[:, columns(h)].astype(jnp.float32).T
         scaled = (turned * lead_row[pl.ds(h, 1), :]).astype(jnp.bfloat16)
-        mine[h] = dot(scaled, g[:, columns(h)], NN).astype(mine.dtype)
-        pair_copy(h).start()
-        return carry
-
-    lax.fori_loop(0, heads, state_step, 0, unroll=2)
+        return dot(scaled, g[:, columns(h)], NN)
+
+    def give_step(i, carry):
+        given[i] = state_of(pair_base + i).astype(given.dtype)
+        pair_copy(i).start()
+        return carry
+
+    def keep_step(i, carry):
+        mine[i] = state_of(own_base + i)
+        return carry
+
+    lax.fori_loop(0, half_heads, give_step, 0, unroll=2)
+    lax.fori_loop(0, half_heads, keep_step, 0, unroll=4)
     fac_copy.wait()
 
     key_at = lax.broadcasted_iota(jnp.int32, (rows, rows), 0)
     query_at = lax.broadcasted_iota(jnp.int32, (rows, rows), 1)
-    allowed = (query_at >= key_at) & (doc_of(query_at) == doc_of(key_at))
+    allowed[...] = jnp.where(
+        (query_at >= key_at) & (doc_of(query_at) == doc_of(key_at)), 1.0, 0.0)
     even = odd == 0
 
-    def head_step(h, carry):
+    def inner(h):
         cols = columns(h)
-        qh, kh, vh, gh = q[:, cols], k[:, cols], v[:, cols], g[:, cols]
+        qh, gh = q[:, cols], g[:, cols]
         along = jnp.broadcast_to(cum[pl.ds(h, 1), :], (rows, rows))
-        weight = jnp.where(allowed, jnp.exp(jnp.minimum(along - along.T, 0.0)), 0.0)
-        mixed_gv = (weight * dot(vh, gh, NT)).astype(jnp.bfloat16)
-        mixed_qk = (weight * dot(kh, qh, NT)).astype(jnp.bfloat16)
-        key_inner = dot(mixed_gv, qh, NN)
-        value_inner = dot(mixed_qk, gh, NN)
+        weight = allowed[...] * jnp.exp(jnp.minimum(along - along.T, 0.0))
+        mixed_gv = (weight * dot(v[:, cols], gh, NT)).astype(jnp.bfloat16)
+        mixed_qk = (weight * dot(k[:, cols], qh, NT)).astype(jnp.bfloat16)
+        key_inner[:, cols] = dot(mixed_gv, qh, NN)
+        value_inner[:, cols] = dot(mixed_qk, gh, NN)
+
+    def apply(h, state_in):
+        cols = columns(h)
         scale = jnp.broadcast_to(tail_row[pl.ds(h, 1), :], (rows, rows)).T
-
-        pair_copy(h).wait_recv()
-        own_state, pair_state = mine[h].astype(jnp.float32), other[h].astype(jnp.float32)
+        dk[:, cols] = (key_inner[:, cols] + scale * dot(v[:, cols], state_in, NT)).astype(dk.dtype)
+        dv[:, cols] = (value_inner[:, cols] + scale * dot(k[:, cols], state_in, NN)).astype(dv.dtype)
+
+    def chain_step(i, carry):
+        h = own_base + i
+        inner(h)
+        inner(pair_base + i)
+        pair_copy(i).wait_recv()
+        own_state, pair_state = mine[i], other[i].astype(jnp.float32)
         own_factor, pair_factor = factor[pl.ds(h, 1), :], factor_other[pl.ds(h, 1), :]
         state_even = jnp.where(even, own_state, pair_state)
         state_odd = jnp.where(even, pair_state, own_state)
         factor_even = jnp.where(even, own_factor, pair_factor)
+        factor_odd = jnp.where(even, pair_factor, own_factor)
+        joined = state_even + factor_even * state_odd
 
         @pl.when(has_after)
         def _():
-            chain_copy(h).wait_recv()
-
-        incoming = jnp.where(has_after, later[h].astype(jnp.float32), 0.0)
+            chain_copy(i).wait_recv()
+
+        incoming = jnp.where(has_after, later[i].astype(jnp.float32), 0.0)
 
         @pl.when(has_before)
         def _():
-            sent[h] = (state_even + factor_even * state_odd
-                       + (own_factor * pair_factor) * incoming).astype(sent.dtype)
-            chain_copy(h).start()
-
-        state_in = jnp.where(even, pair_state + pair_factor * incoming, incoming).astype(jnp.bfloat16)
-        dk[:, cols] = (key_inner + scale * dot(vh, state_in, NT)).astype(dk.dtype)
-        dv[:, cols] = (value_inner + scale * dot(kh, state_in, NN)).astype(dv.dtype)
-        return carry
-
-    lax.fori_loop(0, heads, head_step, 0)
-
-    def drain(h, carry):
-        pair_copy(h).wait_send()
+            sent[i] = (joined + (factor_even * factor_odd) * incoming).astype(sent.dtype)
+            chain_copy(i).start()
+
+        into_even = (state_odd + factor_odd * incoming).astype(jnp.bfloat16)
+        into_odd = incoming.astype(jnp.bfloat16)
+        handed[i] = jnp.where(even, into_odd, into_even)
+        back_copy(i).start()
+        apply(h, jnp.where(even, into_even, into_odd))
+        return carry
+
+    lax.fori_loop(0, half_heads, chain_step, 0)
+
+    def last_step(i, carry):
+        back_copy(i).wait_recv()
+        apply(pair_base + i, back[i])
+        return carry
+
+    lax.fori_loop(0, half_heads, last_step, 0)
+
+    def drain(i, carry):
+        pair_copy(i).wait_send()
+        back_copy(i).wait_send()
 
         @pl.when(has_before)
         def _():
-            chain_copy(h).wait_send()
-
-        return carry
-
-    lax.fori_loop(0, heads, drain, 0)
+            chain_copy(i).wait_send()
+
+        return carry
+
+    lax.fori_loop(0, half_heads, drain, 0)
 
 
 def solution(mesh):
@@ -185,17 +223,22 @@
         in_vmem = pl.BlockSpec(memory_space=pltpu.VMEM)
         wide = pltpu.VMEM((rows, features), jnp.bfloat16)
         small = pltpu.VMEM((heads, rows), jnp.float32)
-        states = pltpu.VMEM((heads, DH, DH), wire)
-        many = pltpu.SemaphoreType.DMA((heads,))
+        half = heads // 2
+        states = pltpu.VMEM((half, DH, DH), wire)
+        kept = pltpu.VMEM((half, DH, DH), jnp.float32)
+        rounded = pltpu.VMEM((half, DH, DH), jnp.bfloat16)
+        total = pltpu.VMEM((rows, features), jnp.float32)
+        square = pltpu.VMEM((rows, rows), jnp.float32)
+        many = pltpu.SemaphoreType.DMA((half,))
         shape = jax.ShapeDtypeStruct((rows, features), jnp.bfloat16)
         return tuple(pl.pallas_call(
             functools.partial(kernel, ctx_count, heads),
             out_shape=(shape, shape),
             in_specs=[pl.BlockSpec(memory_space=pltpu.SMEM), in_vmem] + [anywhere] * 4,
             out_specs=(in_vmem, in_vmem),
-            scratch_shapes=[wide] * 4 + [small] * 5 + [states] * 4 + [
+            scratch_shapes=[wide] * 4 + [small] * 5 + [kept] + [states] * 4 + [rounded] * 2 + [total] * 2 + [square] + [
                 pltpu.SemaphoreType.DMA((4,)), pltpu.SemaphoreType.DMA((2,)), pltpu.SemaphoreType.DMA((2,)),
-                many, many, many, many],
+                many, many, many, many, many, many],
             compiler_params=pltpu.CompilerParams(
                 collective_id=0, has_side_effects=True, vmem_limit_bytes=63 << 20),
         )(doc_ids, log_decay.T, queries, key_rows, value_rows, out_grad))

time: 35.4 us -> 32.3 us (0.912)
  Pallas kernels: 31.8 us -> 28.7 us
    pallas_call x1, Pallas kernels: 31.8 us -> 28.7 us  [per_device(): pl.pallas_call(functools.partial(kernel, ctx_count, heads), out_shape=(sh...]
where the time goes in v2:
time: 32.3 us; the launch traced here: 32.1 us
  Pallas kernels  28.7 us (89%)
  local copies, waits for them, and re-layouts  2.74 us (8%)
  between operations  0.65 us (2%)
    pallas_call x1, Pallas kernels, per_device(): pl.pallas_call(functools.partial(kernel, ctx_count, heads), out_shape=(sh...  28.7 us
    unnamed x4, local copies, waits for them, and re-layouts  2.74 us

profile of v2, /device:TPU:0, one launch (start us, length us, event | category | flops | bytes accessed | tf_op | source)
XLA Modules:
  0.0 32.1 jit_solution(1635667793077796470)
XLA Ops:
  0.6 28.7 %shard_map.77 = (bf16[128,2048]{1,0:T(8,128)(2,1)}, bf16[128,2048]{1,0:T(8,128)(2,1)}) custom-call(s32[16]{0:T(128)} %docs.1, f32[16,128]{1,0:T(8,128)} %bitcast.1, bf16[128,2048]{1,0:T(8,128)(2,1)} %q_hbm.1, bf16[128,2048]{1,0:T(8,128)(2,1)} %k_hbm.1, bf16[128,2048]{1,0:T(8,128)(2,1)} %v_hbm.1, bf16[64,4096]{1,0:T(8,128)(2,1)} %og_hbm.1), custom_call_target="tpu_custom_call" | custom-call | tf_op jit(solution)/shard_map/pallas_call | solution.py:234
  29.4 0.0 copy-start
  29.4 1.9 %copy.10 = bf16[128,2048]{1,0:T(8,128)(2,1)} copy(bf16[128,2048]{1,0:T(8,128)(2,1)} %get-tuple-element.4) | data formatting | bytes 1048576
  31.3 0.0 copy-done
  31.3 0.8 %copy.11 = bf16[128,2048]{1,0:T(8,128)(2,1)} copy(bf16[128,2048]{1,0:T(8,128)(2,1)S(1)} %copy-done) | data formatting | bytes 1048576
Async XLA Ops:
  29.4 2.0 %copy-start = (bf16[128,2048]{1,0:T(8,128)(2,1)S(1)}, bf16[128,2048]{1,0:T(8,128)(2,1)}, u32[]{:S(2)}) copy-start(bf16[128,2048]{1,0:T(8,128)(2,1)} %get-tuple-element.5) | copy-start | bytes 1572868

commit v3 on v2

--- a/solution.py
+++ b/solution.py
@@ -125,15 +125,17 @@
         return dot(scaled, g[:, columns(h)], NN)
 
     def give_step(i, carry):
-        given[i] = state_of(pair_base + i).astype(given.dtype)
-        pair_copy(i).start()
+        for j in range(2):
+            given[2 * i + j] = state_of(pair_base + 2 * i + j).astype(given.dtype)
+        for j in range(2):
+            pair_copy(2 * i + j).start()
         return carry
 
     def keep_step(i, carry):
         mine[i] = state_of(own_base + i)
         return carry
 
-    lax.fori_loop(0, half_heads, give_step, 0, unroll=2)
+    lax.fori_loop(0, half_heads // 2, give_step, 0)
     lax.fori_loop(0, half_heads, keep_step, 0, unroll=4)
     fac_copy.wait()
 
@@ -161,8 +163,6 @@
 
     def chain_step(i, carry):
         h = own_base + i
-        inner(h)
-        inner(pair_base + i)
         pair_copy(i).wait_recv()
         own_state, pair_state = mine[i], other[i].astype(jnp.float32)
         own_factor, pair_factor = factor[pl.ds(h, 1), :], factor_other[pl.ds(h, 1), :]
@@ -187,9 +187,15 @@
         into_odd = incoming.astype(jnp.bfloat16)
         handed[i] = jnp.where(even, into_odd, into_even)
         back_copy(i).start()
+        inner(pair_base + i)
         apply(h, jnp.where(even, into_even, into_odd))
         return carry
 
+    def early_step(i, carry):
+        inner(own_base + i)
+        return carry
+
+    lax.fori_loop(0, half_heads, early_step, 0, unroll=4)
     lax.fori_loop(0, half_heads, chain_step, 0)
 
     def last_step(i, carry):

time: 32.3 us -> 32.2 us (level)
  no operation moved by 1% of the time
where the time goes in v3:
time: 32.2 us; the launch traced here: 32 us
  Pallas kernels  28.6 us (89%)
  local copies, waits for them, and re-layouts  2.74 us (9%)
  between operations  0.65 us (2%)
    pallas_call x1, Pallas kernels, per_device(): pl.pallas_call(functools.partial(kernel, ctx_count, heads), out_shape=(sh...  28.6 us
    unnamed x4, local copies, waits for them, and re-layouts  2.74 us

profile of v3, /device:TPU:0, one launch (start us, length us, event | category | flops | bytes accessed | tf_op | source)
XLA Modules:
  0.0 32.0 jit_solution(14688786946490995524)
XLA Ops:
  0.6 28.6 %shard_map.77 = (bf16[128,2048]{1,0:T(8,128)(2,1)}, bf16[128,2048]{1,0:T(8,128)(2,1)}) custom-call(s32[16]{0:T(128)} %docs.1, f32[16,128]{1,0:T(8,128)} %bitcast.1, bf16[128,2048]{1,0:T(8,128)(2,1)} %q_hbm.1, bf16[128,2048]{1,0:T(8,128)(2,1)} %k_hbm.1, bf16[128,2048]{1,0:T(8,128)(2,1)} %v_hbm.1, bf16[64,4096]{1,0:T(8,128)(2,1)} %og_hbm.1), custom_call_target="tpu_custom_call" | custom-call | tf_op jit(solution)/shard_map/pallas_call | solution.py:240
  29.2 0.0 copy-start
  29.2 1.9 %copy.10 = bf16[128,2048]{1,0:T(8,128)(2,1)} copy(bf16[128,2048]{1,0:T(8,128)(2,1)} %get-tuple-element.4) | data formatting | bytes 1048576
  31.2 0.0 copy-done
  31.2 0.8 %copy.11 = bf16[128,2048]{1,0:T(8,128)(2,1)} copy(bf16[128,2048]{1,0:T(8,128)(2,1)S(1)} %copy-done) | data formatting | bytes 1048576
Async XLA Ops:
  29.2 2.0 %copy-start = (bf16[128,2048]{1,0:T(8,128)(2,1)S(1)}, bf16[128,2048]{1,0:T(8,128)(2,1)}, u32[]{:S(2)}) copy-start(bf16[128,2048]{1,0:T(8,128)(2,1)} %get-tuple-element.5) | copy-start | bytes 1572868

commit v4 on v3

--- a/solution.py
+++ b/solution.py
@@ -20,10 +20,10 @@
 NT = ((1,), (1,))
 
 
-def kernel(ctx_count, heads, docs, decay, q_hbm, k_hbm, v_hbm, og_hbm, dk, dv,
-           q, k, v, g, cum, lead_row, tail_row, factor, factor_other, mine, given, other, sent, later,
+def kernel(ctx_count, heads, docs, decay, q_hbm, k_hbm, v_hbm, og_hbm, dk_hbm, dv_hbm,
+           dk, dv, q, k, v, g, cum, lead_row, tail_row, factor, factor_other, mine, given, other, sent, later,
            handed, back, key_inner, value_inner, allowed,
-           load_sem, swap_sem, fac_sem, pair_send, pair_recv, chain_send, chain_recv, back_send, back_recv):
+           load_sem, swap_sem, fac_sem, pair_send, pair_recv, chain_send, chain_recv, back_send, back_recv, out_sem):
     rows = q.shape[0]
     half = og_hbm.shape[0]
     width = q.shape[1]
@@ -155,11 +155,18 @@
         key_inner[:, cols] = dot(mixed_gv, qh, NN)
         value_inner[:, cols] = dot(mixed_qk, gh, NN)
 
+    def out_copies(h):
+        cols = columns(h)
+        return (pltpu.make_async_copy(dk.at[:, cols], dk_hbm.at[:, cols], out_sem.at[0, h]),
+                pltpu.make_async_copy(dv.at[:, cols], dv_hbm.at[:, cols], out_sem.at[1, h]))
+
     def apply(h, state_in):
         cols = columns(h)
         scale = jnp.broadcast_to(tail_row[pl.ds(h, 1), :], (rows, rows)).T
         dk[:, cols] = (key_inner[:, cols] + scale * dot(v[:, cols], state_in, NT)).astype(dk.dtype)
         dv[:, cols] = (value_inner[:, cols] + scale * dot(k[:, cols], state_in, NN)).astype(dv.dtype)
+        for copy in out_copies(h):
+            copy.start()
 
     def chain_step(i, carry):
         h = own_base + i
@@ -208,6 +215,9 @@
     def drain(i, carry):
         pair_copy(i).wait_send()
         back_copy(i).wait_send()
+        for h in (i, half_heads + i):
+            for copy in out_copies(h):
+                copy.wait()
 
         @pl.when(has_before)
         def _():
@@ -216,6 +226,23 @@
         return carry
 
     lax.fori_loop(0, half_heads, drain, 0)
+
+
+def handover(a_in, b_in, a_out, b_out, a_buf, b_buf, in_sem, out_sem):
+    pieces = a_buf.shape[0] // 32
+    moves = []
+    for i in range(pieces):
+        part = pl.ds(32 * i, 32)
+        for n, (src, buf, dst) in enumerate(((a_in, a_buf, a_out), (b_in, b_buf, b_out))):
+            moves.append((pltpu.make_async_copy(src.at[part, :], buf.at[part, :], in_sem.at[n, i]),
+                          pltpu.make_async_copy(buf.at[part, :], dst.at[part, :], out_sem.at[n, i])))
+    for come, _ in moves:
+        come.start()
+    for come, go in moves:
+        come.wait()
+        go.start()
+    for _, go in moves:
+        go.wait()
 
 
 def solution(mesh):
@@ -237,17 +264,26 @@
         square = pltpu.VMEM((rows, rows), jnp.float32)
         many = pltpu.SemaphoreType.DMA((half,))
         shape = jax.ShapeDtypeStruct((rows, features), jnp.bfloat16)
-        return tuple(pl.pallas_call(
+        key_grad, value_grad = pl.pallas_call(
             functools.partial(kernel, ctx_count, heads),
             out_shape=(shape, shape),
             in_specs=[pl.BlockSpec(memory_space=pltpu.SMEM), in_vmem] + [anywhere] * 4,
-            out_specs=(in_vmem, in_vmem),
-            scratch_shapes=[wide] * 4 + [small] * 5 + [kept] + [states] * 4 + [rounded] * 2 + [total] * 2 + [square] + [
+            out_specs=(anywhere, anywhere),
+            scratch_shapes=[wide] * 6 + [small] * 5 + [kept] + [states] * 4 + [rounded] * 2 + [total] * 2 + [square] + [
                 pltpu.SemaphoreType.DMA((4,)), pltpu.SemaphoreType.DMA((2,)), pltpu.SemaphoreType.DMA((2,)),
-                many, many, many, many, many, many],
+                many, many, many, many, many, many, pltpu.SemaphoreType.DMA((2, heads))],
             compiler_params=pltpu.CompilerParams(
                 collective_id=0, has_side_effects=True, vmem_limit_bytes=63 << 20),
-        )(doc_ids, log_decay.T, queries, key_rows, value_rows, out_grad))
+        )(doc_ids, log_decay.T, queries, key_rows, value_rows, out_grad)
+        pieces = pltpu.SemaphoreType.DMA((2, rows // 32))
+        return tuple(pl.pallas_call(
+            handover,
+            out_shape=(shape, shape),
+            in_specs=[anywhere] * 2,
+            out_specs=(anywhere, anywhere),
+            scratch_shapes=[wide, wide, pieces, pieces],
+            compiler_params=pltpu.CompilerParams(vmem_limit_bytes=63 << 20),
+        )(key_grad, value_grad))
 
     placed = (
         P(("group", "ctx"), "tp"),

time: 32.2 us -> 31.4 us (0.975)
  local copies, waits for them, and re-layouts: 2.74 us -> 0 us
  Pallas kernels: 28.6 us -> 30.5 us
    unnamed x4 -> x0, local copies, waits for them, and re-layouts: 2.74 us -> none
    pallas_call x0 -> x1, Pallas kernels: none -> 2.09 us  [per_device(): pl.pallas_call(handover, out_shape=(shape, shape), in_specs=[anywhere] *...]
where the time goes in v4:
time: 31.4 us; the launch traced here: 31.2 us
  Pallas kernels  30.5 us (97%)
  between operations  0.64 us (2%)
    pallas_call x1, Pallas kernels, per_device(): pl.pallas_call(functools.partial(kernel, ctx_count, heads), out_shape=(sh...  28.4 us
    pallas_call x1, Pallas kernels, per_device(): pl.pallas_call(handover, out_shape=(shape, shape), in_specs=[anywhere] *...  2.09 us

profile of v4, /device:TPU:0, one launch (start us, length us, event | category | flops | bytes accessed | tf_op | source)
XLA Modules:
  0.0 31.2 jit_solution(1411994295148523681)
XLA Ops:
  0.6 28.4 %shard_map.77 = (bf16[128,2048]{1,0:T(8,128)(2,1)}, bf16[128,2048]{1,0:T(8,128)(2,1)}) custom-call(s32[16]{0:T(128)} %docs.1, f32[16,128]{1,0:T(8,128)} %bitcast.1, bf16[128,2048]{1,0:T(8,128)(2,1)} %q_hbm.1, bf16[128,2048]{1,0:T(8,128)(2,1)} %k_hbm.1, bf16[128,2048]{1,0:T(8,128)(2,1)} %v_hbm.1, bf16[64,4096]{1,0:T(8,128)(2,1)} %og_hbm.1), custom_call_target="tpu_custom_call" | custom-call | tf_op jit(solution)/shard_map/pallas_call | solution.py:267
  29.1 2.1 %shard_map.78 = (bf16[128,2048]{1,0:T(8,128)(2,1)}, bf16[128,2048]{1,0:T(8,128)(2,1)}) custom-call(bf16[128,2048]{1,0:T(8,128)(2,1)} %get-tuple-element.4.a_in, bf16[128,2048]{1,0:T(8,128)(2,1)} %get-tuple-element.5.b_in), custom_call_target="tpu_custom_call" | custom-call | tf_op jit(solution)/shard_map/pallas_call | solution.py:279

commit v5 on v4

--- a/solution.py
+++ b/solution.py
@@ -22,7 +22,7 @@
 
 def kernel(ctx_count, heads, docs, decay, q_hbm, k_hbm, v_hbm, og_hbm, dk_hbm, dv_hbm,
            dk, dv, q, k, v, g, cum, lead_row, tail_row, factor, factor_other, mine, given, other, sent, later,
-           handed, back, key_inner, value_inner, allowed,
+           handed, back, held, key_inner, value_inner, allowed,
            load_sem, swap_sem, fac_sem, pair_send, pair_recv, chain_send, chain_recv, back_send, back_recv, out_sem):
     rows = q.shape[0]
     half = og_hbm.shape[0]
@@ -165,8 +165,6 @@
         scale = jnp.broadcast_to(tail_row[pl.ds(h, 1), :], (rows, rows)).T
         dk[:, cols] = (key_inner[:, cols] + scale * dot(v[:, cols], state_in, NT)).astype(dk.dtype)
         dv[:, cols] = (value_inner[:, cols] + scale * dot(k[:, cols], state_in, NN)).astype(dv.dtype)
-        for copy in out_copies(h):
-            copy.start()
 
     def chain_step(i, carry):
         h = own_base + i
@@ -195,7 +193,7 @@
         handed[i] = jnp.where(even, into_odd, into_even)
         back_copy(i).start()
         inner(pair_base + i)
-        apply(h, jnp.where(even, into_even, into_odd))
+        held[i] = jnp.where(even, into_even, into_odd)
         return carry
 
     def early_step(i, carry):
@@ -204,10 +202,22 @@
 
     lax.fori_loop(0, half_heads, early_step, 0, unroll=4)
     lax.fori_loop(0, half_heads, chain_step, 0)
+
+    def own_step(i, carry):
+        for j in range(2):
+            apply(own_base + 2 * i + j, held[2 * i + j])
+        for j in range(2):
+            for copy in out_copies(own_base + 2 * i + j):
+                copy.start()
+        return carry
+
+    lax.fori_loop(0, half_heads // 2, own_step, 0)
 
     def last_step(i, carry):
         back_copy(i).wait_recv()
         apply(pair_base + i, back[i])
+        for copy in out_copies(pair_base + i):
+            copy.start()
         return carry
 
     lax.fori_loop(0, half_heads, last_step, 0)
@@ -269,7 +279,7 @@
             out_shape=(shape, shape),
             in_specs=[pl.BlockSpec(memory_space=pltpu.SMEM), in_vmem] + [anywhere] * 4,
             out_specs=(anywhere, anywhere),
-            scratch_shapes=[wide] * 6 + [small] * 5 + [kept] + [states] * 4 + [rounded] * 2 + [total] * 2 + [square] + [
+            scratch_shapes=[wide] * 6 + [small] * 5 + [kept] + [states] * 4 + [rounded] * 3 + [total] * 2 + [square] + [
                 pltpu.SemaphoreType.DMA((4,)), pltpu.SemaphoreType.DMA((2,)), pltpu.SemaphoreType.DMA((2,)),
                 many, many, many, many, many, many, pltpu.SemaphoreType.DMA((2, heads))],
             compiler_params=pltpu.CompilerParams(

time: 31.4 us -> 31.4 us (level)
  no operation moved by 1% of the time
where the time goes in v5:
time: 31.4 us; the launch traced here: 31.2 us
  Pallas kernels  30.5 us (97%)
  between operations  0.64 us (2%)
    pallas_call x1, Pallas kernels, per_device(): pl.pallas_call(functools.partial(kernel, ctx_count, heads), out_shape=(sh...  28.4 us
    pallas_call x1, Pallas kernels, per_device(): pl.pallas_call(handover, out_shape=(shape, shape), in_specs=[anywhere] *...  2.09 us

profile of v5, /device:TPU:0, one launch (start us, length us, event | category | flops | bytes accessed | tf_op | source)
XLA Modules:
  0.0 31.2 jit_solution(102790650968002883)
XLA Ops:
  0.6 28.4 %shard_map.77 = (bf16[128,2048]{1,0:T(8,128)(2,1)}, bf16[128,2048]{1,0:T(8,128)(2,1)}) custom-call(s32[16]{0:T(128)} %docs.1, f32[16,128]{1,0:T(8,128)} %bitcast.1, bf16[128,2048]{1,0:T(8,128)(2,1)} %q_hbm.1, bf16[128,2048]{1,0:T(8,128)(2,1)} %k_hbm.1, bf16[128,2048]{1,0:T(8,128)(2,1)} %v_hbm.1, bf16[64,4096]{1,0:T(8,128)(2,1)} %og_hbm.1), custom_call_target="tpu_custom_call" | custom-call | tf_op jit(solution)/shard_map/pallas_call | solution.py:277
  29.1 2.1 %shard_map.78 = (bf16[128,2048]{1,0:T(8,128)(2,1)}, bf16[128,2048]{1,0:T(8,128)(2,1)}) custom-call(bf16[128,2048]{1,0:T(8,128)(2,1)} %get-tuple-element.4.a_in, bf16[128,2048]{1,0:T(8,128)(2,1)} %get-tuple-element.5.b_in), custom_call_target="tpu_custom_call" | custom-call | tf_op jit(solution)/shard_map/pallas_call | solution.py:289

commit v6 on v5

--- a/solution.py
+++ b/solution.py
@@ -58,11 +58,17 @@
 
     pl.semaphore_wait(barrier, 2 + has_before.astype(jnp.int32) + has_after.astype(jnp.int32))
 
-    swap = pltpu.make_async_remote_copy(
-        src_ref=og_hbm.at[:, pl.ds(pl.multiple_of((1 - tp) * width, width), width)],
-        dst_ref=g.at[own_rows, :], send_sem=swap_sem.at[0], recv_sem=swap_sem.at[1],
-        device_id=core, device_id_type=MESH)
-    swap.start()
+    part = width // 2
+    swaps = []
+    for n, place in enumerate((1 - odd, odd)):
+        theirs = pl.ds(pl.multiple_of((1 - tp) * width + place * part, part), part)
+        swaps.append(pltpu.make_async_remote_copy(
+            src_ref=og_hbm.at[:, theirs],
+            dst_ref=g.at[own_rows, pl.ds(pl.multiple_of(place * part, part), part)],
+            send_sem=swap_sem.at[0, n], recv_sem=swap_sem.at[1, n],
+            device_id=core, device_id_type=MESH))
+    for swap in swaps:
+        swap.start()
 
     blocks = rows // BLOCK
     doc_list = [docs[ctx * blocks + b] for b in range(blocks)]
@@ -115,9 +121,9 @@
     def columns(h):
         return pl.ds(pl.multiple_of(h * DH, DH), DH)
 
-    for copy in loads:
-        copy.wait()
-    swap.wait()
+    loads[0].wait()
+    loads[3].wait()
+    swaps[0].wait()
 
     def state_of(h):
         turned = q[:, columns(h)].astype(jnp.float32).T
@@ -136,6 +142,9 @@
         return carry
 
     lax.fori_loop(0, half_heads // 2, give_step, 0)
+    swaps[1].wait()
+    loads[1].wait()
+    loads[2].wait()
     lax.fori_loop(0, half_heads, keep_step, 0, unroll=4)
     fac_copy.wait()
 
@@ -280,7 +289,7 @@
             in_specs=[pl.BlockSpec(memory_space=pltpu.SMEM), in_vmem] + [anywhere] * 4,
             out_specs=(anywhere, anywhere),
             scratch_shapes=[wide] * 6 + [small] * 5 + [kept] + [states] * 4 + [rounded] * 3 + [total] * 2 + [square] + [
-                pltpu.SemaphoreType.DMA((4,)), pltpu.SemaphoreType.DMA((2,)), pltpu.SemaphoreType.DMA((2,)),
+                pltpu.SemaphoreType.DMA((4,)), pltpu.SemaphoreType.DMA((2, 2)), pltpu.SemaphoreType.DMA((2,)),
                 many, many, many, many, many, many, pltpu.SemaphoreType.DMA((2, heads))],
             compiler_params=pltpu.CompilerParams(
                 collective_id=0, has_side_effects=True, vmem_limit_bytes=63 << 20),

time: 31.4 us -> 31.2 us (level)
  no operation moved by 1% of the time
where the time goes in v6:
time: 31.2 us; the launch traced here: 31 us
  Pallas kernels  30.4 us (97%)
  between operations  0.64 us (2%)
    pallas_call x1, Pallas kernels, per_device(): pl.pallas_call(functools.partial(kernel, ctx_count, heads), out_shape=(sh...  28.3 us
    pallas_call x1, Pallas kernels, per_device(): pl.pallas_call(handover, out_shape=(shape, shape), in_specs=[anywhere] *...  2.09 us

profile of v6, /device:TPU:0, one launch (start us, length us, event | category | flops | bytes accessed | tf_op | source)
XLA Modules:
  0.0 31.0 jit_solution(8533044230931468166)
XLA Ops:
  0.6 28.3 %shard_map.77 = (bf16[128,2048]{1,0:T(8,128)(2,1)}, bf16[128,2048]{1,0:T(8,128)(2,1)}) custom-call(s32[16]{0:T(128)} %docs.1, f32[16,128]{1,0:T(8,128)} %bitcast.1, bf16[128,2048]{1,0:T(8,128)(2,1)} %q_hbm.1, bf16[128,2048]{1,0:T(8,128)(2,1)} %k_hbm.1, bf16[128,2048]{1,0:T(8,128)(2,1)} %v_hbm.1, bf16[64,4096]{1,0:T(8,128)(2,1)} %og_hbm.1), custom_call_target="tpu_custom_call" | custom-call | tf_op jit(solution)/shard_map/pallas_call | solution.py:286
  28.9 2.1 %shard_map.78 = (bf16[128,2048]{1,0:T(8,128)(2,1)}, bf16[128,2048]{1,0:T(8,128)(2,1)}) custom-call(bf16[128,2048]{1,0:T(8,128)(2,1)} %get-tuple-element.4.a_in, bf16[128,2048]{1,0:T(8,128)(2,1)} %get-tuple-element.5.b_in), custom_call_target="tpu_custom_call" | custom-call | tf_op jit(solution)/shard_map/pallas_call | solution.py:298
